TPU v7x, 32 devices: a whole 2x2x4 slice. The times are simulated.
32 devices in a mesh: groups: 2 (over y), db: 4 (over x, core), cand: 4 (over z).
Axes of the slice: x: 2, y: 2, z: 4, core: 2. Of those that a mesh axis runs over, the one named last changes fastest.
Arguments:
- coords: float32 [3, 128, 64], P(None, ('groups', 'db', 'cand')), parts along dimension 1, may hold values from 0 to 1
- species: int32 [128, 64], P(('groups', 'db', 'cand')), parts along dimension 0, may hold values from 0 to 88
- miller: int32 [3, 4096], replicated, may hold values from -8 to 8
- offsets: int32 [4096], replicated, may hold values from 0 to 1023
- form_amps: float32 [89, 4], replicated, may hold values from 0.5 to 6
- form_decay: float32 [89, 4], replicated, may hold values from 0.2 to 20
- ref_patterns: bfloat16 [65536, 1024], P(('db', 'cand')), may hold values from -6 to 6
Outputs:
- scores: bfloat16 [128, 65536], P('groups', ('db', 'cand')), parts along dimension 0
There are 2 independent parts, one for each index of `groups`. A program takes and returns all parts, laid end to end along the dimension named above; an argument that names none is the same for every part. Nothing has to cross between parts.
All inputs are finite; a program needn't handle non-finite values.
Results may differ from a plain program's by a relative error of at most 0.0071.
Values may be sent and summed in bfloat16 or wider, within the bound.
No kernel may reach another device: no remote copies, remote signals or barrier semaphores. Data moves between devices by JAX's collectives and lax.ppermute only.
A program may use at most 64 MiB of HBM per device.

v0:
```python
import jax
import jax.numpy as jnp
from jax import lax
from jax.sharding import PartitionSpec as P

EPSILON = 1e-06
Q_SCALE = 0.0025
PEAK_WIDTH = 0.5
TWO_PI = 6.283185307179586


def form_table(indices, form_amps, form_decay):
    q_square = (
        indices[0] * indices[0] + indices[1] * indices[1] + indices[2] * indices[2]
    ) * Q_SCALE
    result = jnp.zeros((form_amps.shape[0], indices.shape[1]), jnp.float32)
    for term in range(4):
        result = result + form_amps[:, term : term + 1] * jnp.exp(
            -form_decay[:, term : term + 1] * q_square[None, :]
        )
    return result.astype(jnp.bfloat16)


def structure(atom_coords, atom_species, indices, centres, form_amps, form_decay, nbins):
    count = atom_coords.shape[1]
    atoms = atom_coords.shape[2]
    table = form_table(indices, form_amps, form_decay)
    kinds = jnp.arange(form_amps.shape[0], dtype=jnp.float32)
    onehot = (atom_species.reshape(-1)[:, None] == kinds[None, :]).astype(jnp.bfloat16)
    weights = jnp.dot(onehot, table, preferred_element_type=jnp.float32).reshape(
        count, atoms, indices.shape[1]
    )
    phases = TWO_PI * (
        atom_coords[0][:, :, None] * indices[0][None, None, :]
        + atom_coords[1][:, :, None] * indices[1][None, None, :]
        + atom_coords[2][:, :, None] * indices[2][None, None, :]
    )
    real_part = jnp.sum(weights * jnp.cos(phases), axis=1)
    imag_part = jnp.sum(weights * jnp.sin(phases), axis=1)
    intensity = (real_part * real_part + imag_part * imag_part).astype(jnp.bfloat16)
    bin_grid = jnp.arange(nbins, dtype=jnp.float32)
    distance = (bin_grid[None, :] - centres[:, None]) / PEAK_WIDTH
    profile = jnp.exp(-0.5 * distance * distance).astype(jnp.bfloat16)
    return jnp.dot(intensity, profile, preferred_element_type=jnp.float32)


def standardize(rows):
    row_mean = jnp.mean(rows, axis=1, keepdims=True)
    centered = rows - row_mean
    spread = jnp.sqrt(jnp.mean(centered * centered, axis=1, keepdims=True) + EPSILON)
    return (centered / spread).astype(jnp.bfloat16)


def per_device(coords, species, miller, offsets, form_amps, form_decay, ref_patterns):
    nbins = ref_patterns.shape[1]
    ref_z = standardize(ref_patterns.astype(jnp.float32))
    scale_back = 1.0 / jnp.sqrt(jnp.float32(nbins))
    pattern = structure(
        coords,
        species.astype(jnp.float32),
        miller.astype(jnp.float32),
        offsets.astype(jnp.float32),
        form_amps,
        form_decay,
        nbins,
    )
    cand_z = standardize(pattern)
    product = lax.dot_general(
        lax.all_gather(cand_z, ("db", "cand"), axis=0, tiled=True),
        ref_z,
        (((1,), (1,)), ((), ())),
        preferred_element_type=jnp.float32,
    )
    scores = product * scale_back
    return scores.astype(jnp.bfloat16)


def solution(mesh):
    in_specs = (
        P(None, ("groups", "db", "cand"), None),
        P(("groups", "db", "cand"), None),
        P(),
        P(),
        P(),
        P(),
        P(("db", "cand"), None),
    )
    out_specs = P("groups", ("db", "cand"))
    return jax.shard_map(
        per_device, mesh=mesh, in_specs=in_specs, out_specs=out_specs, check_vma=False
    )
```

profile of v0, /device:TPU:0, one launch (start us, length us, event | category | flops | bytes accessed | tf_op | source)
XLA Modules:
  0.0 74.7 jit_solution(15144540133896257717)
XLA Ops:
  0.0 0.7 convert_element_type.31
  0.7 0.1 eq.15
  0.8 0.8 %negate_bitcast_fusion.3 = (f32[89]{0:T(128)S(1)}, f32[89]{0:T(128)S(1)}, f32[89]{0:T(128)S(1)}, f32[89]{0:T(128)S(1)}, f32[89]{0:T(128)S(1)}, /*index=5*/f32[89]{0:T(128)S(1)}, f32[89]{0:T(128)S(1)}, f32[89]{0:T(128)S(1)}) fusion(f32[89,4]{0,1:T(4,128)} %param.12, f32[89,4]{0,1:T(4,128)} %param.11), kind=kLoop, calls=%fused_computation.44 | loop fusion | flops 356 | bytes 5696 | tf_op jit(solution)/shard_map/mul | solution.py:19
  1.6 0.7 slice_bitcast_fusion.2
  2.3 0.7 convert_element_type.35
  3.1 0.0 copy-start
  3.1 4.7 %convert_reduce_fusion = f32[4096]{0:T(1024)S(1)} fusion(bf16[4096,1024]{1,0:T(8,128)(2,1)} %param.13), kind=kLoop, calls=%fused_computation.1 | loop fusion | flops 8384512 | bytes 8404992 | tf_op jit(solution)/shard_map/reduce_sum | solution.py:48
  7.8 1.1 %copy-done = bf16[4096,1024]{1,0:T(8,128)(2,1)S(1)} copy-done((bf16[4096,1024]{1,0:T(8,128)(2,1)S(1)}, bf16[4096,1024]{1,0:T(8,128)(2,1)}, u32[]{:S(2)}) %copy-start) | copy-done | bytes 8388632
  8.8 0.0 copy-start.1
  8.8 2.8 %fusion.2 = f32[4096]{0:T(1024)S(1)} fusion(bf16[4096,1024]{1,0:T(8,128)(2,1)S(1)} %copy-done, f32[4096]{0:T(1024)S(1)} %broadcast_multiply_fusion), kind=kLoop, calls=%fused_computation.4 | loop fusion | flops 16773120 | bytes 8421376 | tf_op jit(solution)/shard_map/reduce_sum | solution.py:50
  11.6 0.0 copy-done.1
  11.7 0.1 add_multiply_fusion.1
  11.7 17.9 %multiply_reduce_fusion.1 = (f32[4,4096]{1,0:T(4,128)S(1)}, f32[4,4096]{1,0:T(4,128)S(1)}) fusion(f32[4096]{0:T(1024)S(1)} %bitcast.33, f32[4,64]{1,0:T(4,128)S(1)} %get-tuple-element.12, f32[4096]{0:T(1024)S(1)} %bitcast.34, f32[4,64]{1,0:T(4,128)S(1)} %get-tuple-element.13, f32[4096]{0:T(1024)S(1)} %bitcast.35, f32[4,64]{1,0:T(4,128)S(1)} %get-tuple-element.11, ...), kind=kOutput, calls=%fused_computation.12 | convolution fusion | flops 201496832 | bytes 203552 | tf_op jit(solution)/shard_map/dot_general | solution.py:30
  29.6 3.8 %fusion.27 = (f32[4]{0:T(128)S(1)}, f32[4,1024]{1,0:T(4,128)S(1)}) fusion(f32[4096]{0:T(1024)S(1)} %convert_element_type.35, f32[4,4096]{1,0:T(4,128)S(1)} %get-tuple-element.6, f32[4,4096]{1,0:T(4,128)S(1)} %get-tuple-element.5), kind=kOutput, calls=%fused_computation.49 | convolution fusion | flops 54595580 | bytes 163856 | tf_op jit(solution)/shard_map/dot_general | solution.py:44
  33.4 0.2 multiply_reduce_fusion.2
  33.6 0.1 fusion.24
  33.7 35.0 %all-gather = bf16[16,4,1024]{2,1,0:T(4,128)(2,1)S(1)} all-gather(bf16[1,4,1024]{2,1,0:T(4,128)(2,1)S(1)} %fusion.24), channel_id=1, replica_groups=mesh['groups'=2,'db'=4,'cand'=4] {'db','cand'}, dimensions={0}, use_global_device_ids=true | all-gather | bytes 139264 | tf_op jit(solution)/shard_map/all_gather | solution.py:69
  68.7 6.0 %fusion.10 = bf16[64,4096]{1,0:T(8,128)(2,1)} fusion(bf16[64,1024]{1,0:T(8,128)(2,1)S(1)} %reshape.37, bf16[4096,1024]{1,0:T(8,128)(2,1)} %param.13, f32[4096]{0:T(1024)S(1)} %add_sqrt_fusion, f32[4096]{0:T(1024)S(1)} %broadcast_multiply_fusion), kind=kOutput, calls=%fused_computation.10 | convolution fusion | flops 554172416 | bytes 9076736 | tf_op jit(solution)/shard_map/dot_general | solution.py:68
  (6 shorter events, 0.1 us)
Async XLA Ops:
  3.1 5.8 %copy-start = (bf16[4096,1024]{1,0:T(8,128)(2,1)S(1)}, bf16[4096,1024]{1,0:T(8,128)(2,1)}, u32[]{:S(2)}) copy-start(bf16[4096,1024]{1,0:T(8,128)(2,1)} %param.13) | copy-start | bytes 25165828
  8.8 2.8 %copy-start.1 = (s32[3,4096]{1,0:T(4,128)S(1)}, s32[3,4096]{1,0:T(4,128)}, u32[]{:S(2)}) copy-start(s32[3,4096]{1,0:T(4,128)} %param.9) | copy-start | bytes 147460
where the time goes:
time: 75 us; the launch traced here: 74.7 us
  blocking collectives  35 us (47%)
  matrix products  27.7 us (37%)
  other arithmetic  10.1 us (13%)
  local copies, waits for them, and re-layouts  1.9 us (3%)
    all_gather x1, blocking collectives, per_device(): lax.all_gather(cand_z, ('db', 'cand'), axis=0, tiled=True)  35 us
    dot_general x1, matrix products, structure(): jnp.dot(onehot, table, preferred_element_type=jnp.float32)  17.9 us
    dot_general x1, matrix products, per_device(): lax.dot_general(lax.all_gather(cand_z, ('db', 'cand'), axis=0, tiled=True...  5.99 us
    reduce_sum x1, other arithmetic, standardize(): row_mean = jnp.mean(rows, axis=1, keepdims=True)  4.7 us
    dot_general x1, matrix products, structure(): return jnp.dot(intensity, profile, preferred_element_type=jnp.float32)  3.82 us
    reduce_sum x2, other arithmetic, standardize(): jnp.mean(centered * centered, axis=1, keepdims=True) + EPSILON  2.97 us

commit v1 on v0

--- a/solution.py
+++ b/solution.py
@@ -7,6 +7,18 @@
 Q_SCALE = 0.0025
 PEAK_WIDTH = 0.5
 TWO_PI = 6.283185307179586
+
+
+def collect(x, axis, dim):
+    ways, here = (lax.axis_size(axis), lax.axis_index(axis))
+    grown, reach = (x, 1)
+    while reach < ways:
+        theirs = lax.ppermute(grown, axis, [(d, d ^ reach) for d in range(ways)])
+        mine_first = jnp.concatenate([grown, theirs], axis=dim)
+        theirs_first = jnp.concatenate([theirs, grown], axis=dim)
+        grown = jnp.where(here & reach == 0, mine_first, theirs_first)
+        reach = 2 * reach
+    return grown
 
 
 def form_table(indices, form_amps, form_decay):
@@ -66,7 +78,7 @@
     )
     cand_z = standardize(pattern)
     product = lax.dot_general(
-        lax.all_gather(cand_z, ("db", "cand"), axis=0, tiled=True),
+        collect(cand_z, ("db", "cand"), 0),
         ref_z,
         (((1,), (1,)), ((), ())),
         preferred_element_type=jnp.float32,

time: 75 us -> 52 us (0.69)
  blocking collectives: 35 us -> 0 us
  starting transfers between devices: 0 us -> 8.11 us
  waiting for transfers between devices: 0 us -> 4.9 us
  local copies, waits for them, and re-layouts: 1.9 us -> 0.81 us
    all_gather x1 -> x0, blocking collectives: 35 us -> none  [per_device(): lax.all_gather(cand_z, ('db', 'cand'), axis=0, tiled=True)]
    ppermute x0 -> x4, starting transfers between devices: none -> 8.11 us  [collect(): theirs = lax.ppermute(grown, axis, [(d, d ^ reach) for d in range(ways)])]
    ppermute x0 -> x4, waiting for transfers between devices: none -> 4.9 us  [collect(): theirs = lax.ppermute(grown, axis, [(d, d ^ reach) for d in range(ways)])]
    reduce_sum x1, other arithmetic: 4.7 us -> 1.17 us  [standardize(): row_mean = jnp.mean(rows, axis=1, keepdims=True)]
    reduce_sum x2, other arithmetic: 2.97 us -> 5.61 us  [standardize(): jnp.mean(centered * centered, axis=1, keepdims=True) + EPSILON]
    unnamed x5 -> x4, local copies, waits for them, and re-layouts: 1.09 us -> 0.01 us
    convert_element_type x1, other arithmetic: 0.01 us -> 0.85 us  [per_device(): miller.astype(jnp.float32)]
  transfers between devices with their start and end apart: 0 -> 4, of which waited for: 0 -> 3; matrix products, arithmetic and copies ran while one was open for 0% -> 13% of each run, Pallas kernels for 0% -> 0%
where the time goes in v1:
time: 52 us; the launch traced here: 51.7 us
  matrix products  27.7 us (53%)
  other arithmetic  10.1 us (19%)
  starting transfers between devices  8.11 us (16%)
  waiting for transfers between devices  4.9 us (9%)
  local copies, waits for them, and re-layouts  0.81 us (2%)
    dot_general x1, matrix products, structure(): jnp.dot(onehot, table, preferred_element_type=jnp.float32)  17.8 us
    ppermute x4, starting transfers between devices, collect(): theirs = lax.ppermute(grown, axis, [(d, d ^ reach) for d in range(ways)])  8.11 us
    dot_general x1, matrix products, per_device(): lax.dot_general(collect(cand_z, ('db', 'cand'), 0), ref_z, (((1,), (1,)),...  6 us
    reduce_sum x2, other arithmetic, standardize(): jnp.mean(centered * centered, axis=1, keepdims=True) + EPSILON  5.61 us
    ppermute x4, waiting for transfers between devices, collect(): theirs = lax.ppermute(grown, axis, [(d, d ^ reach) for d in range(ways)])  4.9 us
    dot_general x1, matrix products, structure(): return jnp.dot(intensity, profile, preferred_element_type=jnp.float32)  3.82 us
    reduce_sum x1, other arithmetic, standardize(): row_mean = jnp.mean(rows, axis=1, keepdims=True)  1.17 us
  transfers between devices with their start and end apart: 4, of which 3 were waited for; matrix products, arithmetic and copies ran while one was open for 13% of the time, Pallas kernels for 0%

profile of v1, /device:TPU:0, one launch (start us, length us, event | category | flops | bytes accessed | tf_op | source)
XLA Modules:
  0.0 51.7 jit_solution(5566678605497080333)
XLA Ops:
  0.0 0.7 %convert_element_type.31 = f32[4,64]{1,0:T(4,128)S(1)} convert(s32[4,64]{1,0:T(4,128)} %param.8) | non-fusion elementwise | flops 256 | bytes 2048 | tf_op jit(solution)/shard_map/convert_element_type | solution.py:72
  0.7 0.1 eq.31
  0.8 0.7 %slice_bitcast_fusion.2 = (f32[4,64]{1,0:T(4,128)S(1)}, f32[4,64]{1,0:T(4,128)S(1)}, f32[4,64]{1,0:T(4,128)S(1)}) fusion(f32[3,4,64]{2,1,0:T(4,128)} %param.7), kind=kLoop, calls=%fused_computation.45 | loop fusion | bytes 6144 | tf_op jit(solution)/shard_map/mul | solution.py:46
  1.5 0.7 %convert_element_type.35 = f32[4096]{0:T(1024)S(1)} convert(s32[4096]{0:T(1024)} %param.10) | non-fusion elementwise | flops 4096 | bytes 32768 | tf_op jit(solution)/shard_map/convert_element_type | solution.py:74
  2.2 0.9 %convert_element_type.32 = f32[3,4096]{1,0:T(4,128)S(1)} convert(s32[3,4096]{1,0:T(4,128)} %param.9) | non-fusion elementwise | flops 12288 | bytes 98304 | tf_op jit(solution)/shard_map/convert_element_type | solution.py:73
  3.1 0.1 add_multiply_fusion.1
  3.1 0.8 %negate_bitcast_fusion.3 = (f32[89]{0:T(128)S(1)}, f32[89]{0:T(128)S(1)}, f32[89]{0:T(128)S(1)}, f32[89]{0:T(128)S(1)}, f32[89]{0:T(128)S(1)}, /*index=5*/f32[89]{0:T(128)S(1)}, f32[89]{0:T(128)S(1)}, f32[89]{0:T(128)S(1)}) fusion(f32[89,4]{0,1:T(4,128)} %param.12, f32[89,4]{0,1:T(4,128)} %param.11), kind=kLoop, calls=%fused_computation.53 | loop fusion | flops 356 | bytes 5696 | tf_op jit(solution)/shard_map/mul | solution.py:31
  4.0 17.8 %multiply_reduce_fusion.1 = (f32[4,4096]{1,0:T(4,128)S(1)}, f32[4,4096]{1,0:T(4,128)S(1)}) fusion(f32[4096]{0:T(1024)S(1)} %bitcast.32, f32[4,64]{1,0:T(4,128)S(1)} %get-tuple-element.12, f32[4096]{0:T(1024)S(1)} %bitcast.33, f32[4,64]{1,0:T(4,128)S(1)} %get-tuple-element.13, f32[4096]{0:T(1024)S(1)} %bitcast.34, f32[4,64]{1,0:T(4,128)S(1)} %get-tuple-element.11, ...), kind=kOutput, calls=%fused_computation.12 | convolution fusion | flops 201496832 | bytes 203552 | tf_op jit(solution)/shard_map/dot_general | solution.py:42
  21.8 0.0 slice-start
  21.8 0.0 slice-start.1
  21.8 3.8 %fusion.33 = (f32[4]{0:T(128)S(1)}, f32[4,1024]{1,0:T(4,128)S(1)}) fusion(f32[4096]{0:T(1024)S(1)} %convert_element_type.35, f32[4,4096]{1,0:T(4,128)S(1)} %get-tuple-element.6, f32[4,4096]{1,0:T(4,128)S(1)} %get-tuple-element.5), kind=kOutput, calls=%fused_computation.59 | convolution fusion | flops 54595580 | bytes 163856 | tf_op jit(solution)/shard_map/dot_general | solution.py:56
  25.7 0.2 multiply_reduce_fusion.2
  25.9 0.1 divide_convert_fusion
  26.0 3.0 %collective-permute-start = (bf16[4,1024]{1,0:T(4,128)(2,1)S(1)}, bf16[4,1024]{1,0:T(4,128)(2,1)S(1)}, u32[]{:S(2)}, u32[]{:S(2)}) collective-permute-start(bf16[4,1024]{1,0:T(4,128)(2,1)S(1)} %divide_convert_fusion), channel_id=1, source_target_pairs={{0,1},{1,0},{2,3},{3,2},{4,5},{5,4},{6,7},{7,6},{8,9},{9,8},{10,11... | collective-permute-start | bytes 24584 | tf_op jit(solution)/shard_map/ppermute | solution.py:16
  29.0 0.0 slice-done
  29.0 0.0 slice-done.1
  29.0 1.2 %convert_reduce_fusion = f32[4096]{0:T(1024)S(1)} fusion(bf16[4096,1024]{1,0:T(8,128)(2,1)S(1)} %bitcast.30), kind=kLoop, calls=%fused_computation.1 | loop fusion | flops 8384512 | bytes 8404992 | tf_op jit(solution)/shard_map/reduce_sum | solution.py:60
  30.2 0.5 collective-permute-done
  30.7 3.1 %collective-permute-start.1 = (bf16[8,1024]{1,0:T(8,128)(2,1)S(1)}, bf16[8,1024]{1,0:T(8,128)(2,1)S(1)}, u32[]{:S(2)}, u32[]{:S(2)}) collective-permute-start(bf16[8,1024]{1,0:T(8,128)(2,1)S(1)} %maximum_select_fusion.4), channel_id=1, source_target_pairs={{0,2},{1,3},{2,0},{3,1},{4,6},{5,7},{6,4},{7,5},{8,10},{9,11},{10,... | collective-permute-start | bytes 49160 | tf_op jit(solution)/shard_map/ppermute | solution.py:16
  33.8 1.7 %collective-permute-done.1 = bf16[8,1024]{1,0:T(8,128)(2,1)S(1)} collective-permute-done((bf16[8,1024]{1,0:T(8,128)(2,1)S(1)}, bf16[8,1024]{1,0:T(8,128)(2,1)S(1)}, u32[]{:S(2)}, u32[]{:S(2)}) %collective-permute-start.1) | collective-permute-done | bytes 16416 | tf_op jit(solution)/shard_map/ppermute | solution.py:16
  35.5 0.1 collective-permute-start.2
  35.6 5.4 %fusion.2 = f32[4096]{0:T(1024)S(1)} fusion(bf16[4096,1024]{1,0:T(8,128)(2,1)} %param.13, f32[4096]{0:T(1024)S(1)} %broadcast_multiply_fusion), kind=kLoop, calls=%fused_computation.4 | loop fusion | flops 16773120 | bytes 8421376 | tf_op jit(solution)/shard_map/reduce_sum | solution.py:62
  41.0 0.0 collective-permute-done.2
  41.0 1.9 %collective-permute-start.3 = (bf16[32,1024]{1,0:T(8,128)(2,1)S(1)}, bf16[32,1024]{1,0:T(8,128)(2,1)S(1)}, u32[]{:S(2)}, u32[]{:S(2)}) collective-permute-start(bf16[32,1024]{1,0:T(8,128)(2,1)S(1)} %maximum_select_fusion.2), channel_id=1, source_target_pairs={{0,8},{1,9},{2,10},{3,11},{4,12},{5,13},{6,14},{7,15},{8,0},{9,1},... | collective-permute-start | bytes 196616 | tf_op jit(solution)/shard_map/ppermute | solution.py:16
  42.9 2.7 %collective-permute-done.3 = bf16[32,1024]{1,0:T(8,128)(2,1)S(1)} collective-permute-done((bf16[32,1024]{1,0:T(8,128)(2,1)S(1)}, bf16[32,1024]{1,0:T(8,128)(2,1)S(1)}, u32[]{:S(2)}, u32[]{:S(2)}) %collective-permute-start.3) | collective-permute-done | bytes 65568 | tf_op jit(solution)/shard_map/ppermute | solution.py:16
  45.7 6.0 %fusion.10 = bf16[64,4096]{1,0:T(8,128)(2,1)} fusion(bf16[4096,1024]{1,0:T(8,128)(2,1)} %param.13, f32[4096]{0:T(1024)S(1)} %add_sqrt_fusion, f32[4096]{0:T(1024)S(1)} %broadcast_multiply_fusion, bf16[32,1024]{1,0:T(8,128)(2,1)S(1)} %collective-permute-done.3, bf16[32,1024]{1,0:T(8,128)(2,1)S(1)} %maximum_select_fusion.2, pred[]{:T(512)S(6)} %eq.27), kind=kOutput, calls=%fused_computation.10 | convolution fusion | flops 554762240 | bytes 9076737 | tf_op jit(solution)/shard_map/dot_general | solution.py:80
  (8 shorter events, 0.1 us)
Async XLA Ops:
  21.8 7.2 %slice-start = ((s8[8388608]{0:T(1024)(128)(4,1)}), s8[4194304]{0:T(1024)(128)(4,1)S(1)}, s32[]{:S(2)}) async-start(s8[8388608]{0:T(1024)(128)(4,1)} %bitcast.29), calls=%async_computation | async-start | bytes 8388608
  21.8 7.2 %slice-start.1 = ((s8[8388608]{0:T(1024)(128)(4,1)}), s8[4194304]{0:T(1024)(128)(4,1)S(1)}, s32[]{:S(2)}) async-start(s8[8388608]{0:T(1024)(128)(4,1)} %bitcast.29), calls=%async_computation.1 | async-start | bytes 8388608
  26.0 4.7 %collective-permute-start = (bf16[4,1024]{1,0:T(4,128)(2,1)S(1)}, bf16[4,1024]{1,0:T(4,128)(2,1)S(1)}, u32[]{:S(2)}, u32[]{:S(2)}) collective-permute-start(bf16[4,1024]{1,0:T(4,128)(2,1)S(1)} %divide_convert_fusion), channel_id=1, source_target_pairs={{0,1},{1,0},{2,3},{3,2},{4,5},{5,4},{6,7},{7,6},{8,9},{9,8},{10,11... | collective-permute-start | bytes 24584 | tf_op jit(solution)/shard_map/ppermute | solution.py:16
  30.7 4.8 %collective-permute-start.1 = (bf16[8,1024]{1,0:T(8,128)(2,1)S(1)}, bf16[8,1024]{1,0:T(8,128)(2,1)S(1)}, u32[]{:S(2)}, u32[]{:S(2)}) collective-permute-start(bf16[8,1024]{1,0:T(8,128)(2,1)S(1)} %maximum_select_fusion.4), channel_id=1, source_target_pairs={{0,2},{1,3},{2,0},{3,1},{4,6},{5,7},{6,4},{7,5},{8,10},{9,11},{10,... | collective-permute-start | bytes 49160 | tf_op jit(solution)/shard_map/ppermute | solution.py:16
  35.5 5.5 %collective-permute-start.2 = (bf16[16,1024]{1,0:T(8,128)(2,1)S(1)}, bf16[16,1024]{1,0:T(8,128)(2,1)S(1)}, u32[]{:S(2)}, u32[]{:S(2)}) collective-permute-start(bf16[16,1024]{1,0:T(8,128)(2,1)S(1)} %maximum_select_fusion.3), channel_id=1, source_target_pairs={{0,4},{1,5},{2,6},{3,7},{4,0},{5,1},{6,2},{7,3},{8,12},{9,13},{10,... | collective-permute-start | bytes 98312 | tf_op jit(solution)/shard_map/ppermute | solution.py:16
  41.0 4.6 %collective-permute-start.3 = (bf16[32,1024]{1,0:T(8,128)(2,1)S(1)}, bf16[32,1024]{1,0:T(8,128)(2,1)S(1)}, u32[]{:S(2)}, u32[]{:S(2)}) collective-permute-start(bf16[32,1024]{1,0:T(8,128)(2,1)S(1)} %maximum_select_fusion.2), channel_id=1, source_target_pairs={{0,8},{1,9},{2,10},{3,11},{4,12},{5,13},{6,14},{7,15},{8,0},{9,1},... | collective-permute-start | bytes 196616 | tf_op jit(solution)/shard_map/ppermute | solution.py:16
